TPU v7x, 32 devices: a whole 2x2x4 slice. The times are simulated.
32 devices in a mesh: dp: 8 (over y, x, core), tensor: 4 (over z).
Axes of the slice: x: 2, y: 2, z: 4, core: 2. Of those that a mesh axis runs over, the one named last changes fastest.
Arguments:
- tokens: bfloat16 [16384, 2048], P(('dp', 'tensor'))
- teacher: bfloat16 [16384, 2048], P(('dp', 'tensor')), may hold values from -6 to 6
- valid: int32 [16384], P(('dp', 'tensor')), may hold values from 0 to 1, as said below
- prefix: int32 [16], P('dp'), may hold values from 102 to 512, as said below
- w_query: bfloat16 [2048, 1024], P(None, 'tensor'), may hold values from -0.125 to 0.125
- key_weight: bfloat16 [2048, 256], replicated, may hold values from -0.125 to 0.125
- value_weight: bfloat16 [2048, 256], replicated, may hold values from -0.125 to 0.125
- query_gain: float32 [64], replicated, may hold values from 0.25 to 1.75
- key_gain: float32 [64], replicated, may hold values from 0.25 to 1.75
- w_out: bfloat16 [1024, 2048], P('tensor'), may hold values from -3 to 3
- attn_gain: float32 [2048], replicated, may hold values from 0.25 to 1.75
- ffn_gain: float32 [2048], replicated, may hold values from 0.25 to 1.75
- w_gate: bfloat16 [2048, 5120], P(None, 'tensor'), may hold values from -0.125 to 0.125
- w_up: bfloat16 [2048, 5120], P(None, 'tensor'), may hold values from -0.125 to 0.125
- w_down: bfloat16 [5120, 2048], P('tensor'), may hold values from -0.078125 to 0.078125
Outputs:
- output: bfloat16 [16384, 2048], P(('dp', 'tensor'))
- loss: float32 [], replicated
- grad_tokens: float32 [16384, 2048], P(('dp', 'tensor'))
- grad_query: float32 [2048, 1024], P(None, 'tensor')
- grad_key: float32 [2048, 256], replicated
- grad_value: float32 [2048, 256], replicated
- grad_query_gain: float32 [64], replicated
- grad_key_gain: float32 [64], replicated
- grad_out: float32 [1024, 2048], P('tensor')
- grad_attn_gain: float32 [2048], replicated
- grad_ffn_gain: float32 [2048], replicated
- grad_gate: float32 [2048, 5120], P(None, 'tensor')
- grad_up: float32 [2048, 5120], P(None, 'tensor')
- grad_down: float32 [5120, 2048], P('tensor')
Inputs may be any that keep to these rules, and one draw needn't show every extreme that they name: The first token of every sequence is valid. One sequence has prefix length exactly 512 and another exactly 102.
All inputs are finite; a program needn't handle non-finite values.
Results may differ from a plain program's by a relative error of at most 0.015.
Values may be sent and summed in bfloat16 or wider, within the bound.
A program may use at most 256 MiB of HBM per device.

v0:
```python
import jax
import jax.numpy as jnp
from jax import lax
from jax.sharding import PartitionSpec as P

QUERY_HEADS = 16
KEY_VALUE_HEADS = 4
HEAD_SIZE = 64
SEQ_LEN = 1024
GROUP = QUERY_HEADS // KEY_VALUE_HEADS
EPSILON = 1e-06
BF = jnp.bfloat16
F32 = jnp.float32


def rope_rows(start, rows):
    half = HEAD_SIZE // 2
    frequency = 10000.0 ** (-2.0 * jnp.arange(half, dtype=F32) / HEAD_SIZE)
    angles = (start + jnp.arange(rows)).astype(F32)[:, None] * frequency[None, :]
    cosine = jnp.concatenate([jnp.cos(angles), jnp.cos(angles)], 1)
    sine = jnp.concatenate([jnp.sin(angles), jnp.sin(angles)], 1)
    return (cosine[:, None, :], sine[:, None, :])


def rotate(vector, cosine, sine):
    half = vector.shape[-1] // 2
    turned = jnp.concatenate([-vector[..., half:], vector[..., :half]], -1)
    return vector * cosine + turned * sine


def unrotate(gradient, cosine, sine):
    half = gradient.shape[-1] // 2
    shifted = gradient * sine
    return gradient * cosine + jnp.concatenate([shifted[..., half:], -shifted[..., :half]], -1)


def inv_root(vector):
    return lax.rsqrt(jnp.mean(vector * vector, axis=-1, keepdims=True) + EPSILON)


def norm_back(gradient, source, factor, gain):
    scaled = gradient * gain
    return factor * scaled - source * factor**3 * jnp.mean(scaled * source, axis=-1, keepdims=True)


def dot(a, b):
    return jnp.dot(a, b, preferred_element_type=F32)


def dot_t(a, b):
    return lax.dot_general(a, b, (((1,), (1,)), ((), ())), preferred_element_type=F32)


def t_dot(a, b):
    return lax.dot_general(a, b, (((0,), (0,)), ((), ())), preferred_element_type=F32)


def seen(start, rows, prefix_len):
    row = start + jnp.arange(rows)[:, None]
    col = jnp.arange(SEQ_LEN)[None, :]
    return (col <= row) | (row < prefix_len) & (col < prefix_len)


def attend(q, k, v, start, prefix_len):
    rows = q.shape[0]
    grouped = q.reshape(rows, KEY_VALUE_HEADS, GROUP, HEAD_SIZE)
    scores = jnp.einsum("ikgd,jkd->kgij", grouped, k, preferred_element_type=F32) * HEAD_SIZE ** (
        -0.5
    )
    allowed = seen(start, rows, prefix_len)
    scores = jnp.where(allowed, scores, -1e30)
    top = jnp.max(scores, -1, keepdims=True)
    weights = jnp.where(allowed, jnp.exp(scores - top), 0.0)
    total = jnp.sum(weights, -1, keepdims=True)
    probs = (weights / total).astype(BF)
    attended = jnp.einsum("kgij,jkd->ikgd", probs, v, preferred_element_type=F32)
    return (attended.reshape(rows, QUERY_HEADS * HEAD_SIZE), (top + jnp.log(total))[..., 0])


def attend_back(q, k, v, start, prefix_len, lse, grad):
    rows = q.shape[0]
    scale = HEAD_SIZE ** (-0.5)
    grouped = q.reshape(rows, KEY_VALUE_HEADS, GROUP, HEAD_SIZE)
    scores = jnp.einsum("ikgd,jkd->kgij", grouped, k, preferred_element_type=F32) * scale
    allowed = seen(start, rows, prefix_len)
    probs = jnp.where(allowed, jnp.exp(jnp.where(allowed, scores, -1e30) - lse[..., None]), 0.0)
    heads = grad.reshape(rows, KEY_VALUE_HEADS, GROUP, HEAD_SIZE)
    dprobs = jnp.einsum("ikgd,jkd->kgij", heads, v, preferred_element_type=F32)
    inner = jnp.sum(probs * dprobs, -1, keepdims=True)
    dscores = (probs * (dprobs - inner)).astype(BF)
    dq = jnp.einsum("kgij,jkd->ikgd", dscores, k, preferred_element_type=F32) * scale
    dk = jnp.einsum("kgij,ikgd->jkd", dscores, grouped, preferred_element_type=F32) * scale
    dv = jnp.einsum("kgij,ikgd->jkd", probs.astype(BF), heads, preferred_element_type=F32)
    return (dq.reshape(rows, QUERY_HEADS, HEAD_SIZE), dk, dv)


def sum_small(vector):
    return jnp.sum(lax.all_gather(vector[None], ("dp", "tensor"), axis=0, tiled=True), 0)


def body(
    tokens,
    teacher,
    valid,
    prefix,
    w_query,
    key_weight,
    value_weight,
    query_gain,
    key_gain,
    w_out,
    attn_gain,
    ffn_gain,
    w_gate,
    w_up,
    w_down,
):
    rows, width = tokens.shape
    dp_size, t_size = (lax.axis_size("dp"), lax.axis_size("tensor"))
    dp_at, t_at = (lax.axis_index("dp"), lax.axis_index("tensor"))
    per_seq = SEQ_LEN // rows
    seq_groups = [list(range(g, g + per_seq)) for g in range(0, t_size, per_seq)]
    start = t_at % per_seq * rows
    prefix_len = prefix[t_at // per_seq]
    q_all = QUERY_HEADS * HEAD_SIZE
    kv_all = KEY_VALUE_HEADS * HEAD_SIZE
    q_dev = w_query.shape[1]
    cut = width // dp_size
    count = sum_small(jnp.broadcast_to(jnp.sum(valid).astype(F32), (128,)))[0]
    query_cut = lax.dynamic_slice_in_dim(w_query, dp_at * cut, cut, 0)
    query_full = (
        lax.all_gather(query_cut, ("dp", "tensor"), axis=0, tiled=False)
        .reshape(dp_size, t_size, cut, q_dev)
        .transpose(0, 2, 1, 3)
        .reshape(width, q_all)
    )
    out_rows = w_out.shape[0] // dp_size
    out_cut = lax.dynamic_slice_in_dim(w_out, dp_at * out_rows, out_rows, 0)
    out_full = lax.all_gather(out_cut, ("tensor", "dp"), axis=0, tiled=True)
    source = tokens.astype(F32)
    factor_one = inv_root(source)
    normed = (source * factor_one * attn_gain).astype(BF)
    k_raw = dot(normed, key_weight).reshape(rows, KEY_VALUE_HEADS, HEAD_SIZE)
    v_low = dot(normed, value_weight).astype(BF)
    cosine, sine = rope_rows(start, rows)
    k_factor = inv_root(k_raw)
    k_low = rotate(k_raw * k_factor * key_gain, cosine, sine).astype(BF).reshape(rows, kv_all)
    kv_seq = lax.all_gather(
        jnp.concatenate([k_low, v_low], 1),
        "tensor",
        axis=0,
        tiled=True,
        axis_index_groups=seq_groups,
    )
    k_seq = kv_seq[:, :kv_all].reshape(SEQ_LEN, KEY_VALUE_HEADS, HEAD_SIZE)
    v_seq = kv_seq[:, kv_all:].reshape(SEQ_LEN, KEY_VALUE_HEADS, HEAD_SIZE)
    q_raw = dot(normed, query_full).reshape(rows, QUERY_HEADS, HEAD_SIZE)
    q_factor = inv_root(q_raw)
    q_low = rotate(q_raw * q_factor * query_gain, cosine, sine).astype(BF)
    attended, lse = attend(q_low, k_seq, v_seq, start, prefix_len)
    attended = attended.astype(BF)
    middle = source + dot(attended, out_full)
    factor_two = inv_root(middle)
    normed_two = (middle * factor_two * ffn_gain).astype(BF)
    normed_two_all = lax.all_gather(normed_two, "tensor", axis=0, tiled=True)
    gate = dot(normed_two_all, w_gate)
    up = dot(normed_two_all, w_up)
    sig = jax.nn.sigmoid(gate)
    hidden = (gate * sig * up).astype(BF)
    result = middle + lax.psum_scatter(
        dot(hidden, w_down).astype(BF), "tensor", scatter_dimension=0, tiled=True
    ).astype(F32)
    mask = valid.astype(F32)[:, None]
    error = result - teacher.astype(F32)
    squares = jnp.sum(error * error * mask)
    cot = rows * t_size * dp_size / count * error * mask
    cot_all = lax.all_gather(cot.astype(BF), "tensor", axis=0, tiled=True)
    grad_down = t_dot(hidden, cot_all)
    dhidden = dot_t(cot_all, w_down)
    dgate = (dhidden * up * sig * (1.0 + gate * (1.0 - sig))).astype(BF)
    dup = (dhidden * gate * sig).astype(BF)
    dn2 = lax.psum_scatter(
        (dot_t(dgate, w_gate) + dot_t(dup, w_up)).astype(BF),
        "tensor",
        scatter_dimension=0,
        tiled=True,
    ).astype(F32)
    grad_gate = t_dot(normed_two_all, dgate)
    grad_up = t_dot(normed_two_all, dup)
    grad_gate, grad_up, grad_down = (
        lax.psum(g.astype(BF), "dp").astype(F32) for g in (grad_gate, grad_up, grad_down)
    )
    grad_ffn_gain = jnp.sum(dn2 * middle * factor_two, 0)
    dmiddle = cot + norm_back(dn2, middle, factor_two, ffn_gain)
    da = dmiddle.astype(BF)
    grad_out_t = t_dot(da, attended).astype(BF)
    dattended = dot_t(da, out_full).astype(BF)
    dq_rot, dk_part, dv_part = attend_back(q_low, k_seq, v_seq, start, prefix_len, lse, dattended)
    dkv = lax.psum_scatter(
        jnp.concatenate(
            [dk_part.reshape(SEQ_LEN, kv_all), dv_part.reshape(SEQ_LEN, kv_all)], 1
        ).astype(BF),
        "tensor",
        scatter_dimension=0,
        tiled=True,
        axis_index_groups=seq_groups,
    ).astype(F32)
    dq_normed = unrotate(dq_rot, cosine, sine)
    dk_normed = unrotate(dkv[:, :kv_all].reshape(rows, KEY_VALUE_HEADS, HEAD_SIZE), cosine, sine)
    grad_query_gain = jnp.sum(dq_normed * q_raw * q_factor, (0, 1))
    grad_key_gain = jnp.sum(dk_normed * k_raw * k_factor, (0, 1))
    dq = norm_back(dq_normed, q_raw, q_factor, query_gain).reshape(rows, q_all).astype(BF)
    dk = norm_back(dk_normed, k_raw, k_factor, key_gain).reshape(rows, kv_all).astype(BF)
    dv = dkv[:, kv_all:].astype(BF)
    dn1 = dot_t(dq, query_full) + dot_t(dk, key_weight) + dot_t(dv, value_weight)
    grad_attn_gain = jnp.sum(dn1 * source * factor_one, 0)
    grad_tokens = dmiddle + norm_back(dn1, source, factor_one, attn_gain)
    grad_query = t_dot(normed, dq).astype(BF)
    grad_kv = t_dot(normed, jnp.concatenate([dk, dv], 1)).astype(BF)
    wide = jnp.concatenate([grad_query, grad_out_t, grad_kv], 1)
    wide = lax.psum_scatter(wide, "dp", scatter_dimension=0, tiled=True)
    parts = jnp.concatenate(
        [
            wide[:, : 2 * q_all]
            .reshape(cut, 2, t_size, q_dev)
            .transpose(0, 2, 1, 3)
            .reshape(cut, t_size, 2 * q_dev),
            wide[:, 2 * q_all :].reshape(cut, t_size, 2 * kv_all // t_size),
        ],
        2,
    ).reshape(cut, -1)
    parts = lax.psum_scatter(parts, "tensor", scatter_dimension=1, tiled=True)
    own = lax.all_gather(parts[:, : 2 * q_dev], "dp", axis=0, tiled=True).astype(F32)
    grad_query = own[:, :q_dev]
    grad_out = own[:, q_dev:].T
    kv = (
        lax.all_gather(parts[:, 2 * q_dev :], ("dp", "tensor"), axis=0, tiled=False)
        .reshape(dp_size, t_size, cut, 2 * kv_all // t_size)
        .transpose(0, 2, 1, 3)
        .reshape(width, 2 * kv_all)
        .astype(F32)
    )
    small = sum_small(
        jnp.concatenate(
            [
                grad_attn_gain,
                grad_ffn_gain,
                grad_query_gain,
                grad_key_gain,
                jnp.broadcast_to(squares, (128,)),
            ]
        )
    )
    loss = small[2 * width + 2 * HEAD_SIZE] / (count * width)
    return (
        result.astype(BF),
        loss,
        grad_tokens,
        grad_query,
        kv[:, :kv_all],
        kv[:, kv_all:],
        small[2 * width : 2 * width + HEAD_SIZE],
        small[2 * width + HEAD_SIZE : 2 * width + 2 * HEAD_SIZE],
        grad_out,
        small[:width],
        small[width : 2 * width],
        grad_gate,
        grad_up,
        grad_down,
    )


def solution(mesh):
    rows, cols, whole = (P(("dp", "tensor"), None), P(None, "tensor"), P())
    down = P("tensor", None)
    return jax.shard_map(
        body,
        mesh=mesh,
        in_specs=(
            rows,
            rows,
            P(("dp", "tensor")),
            P("dp"),
            cols,
            whole,
            whole,
            whole,
            whole,
            down,
            whole,
            whole,
            cols,
            cols,
            down,
        ),
        out_specs=(
            rows,
            whole,
            rows,
            cols,
            whole,
            whole,
            whole,
            whole,
            down,
            whole,
            whole,
            cols,
            cols,
            down,
        ),
        check_vma=False,
    )
```

profile of v0, /device:TPU:0, one launch (start us, length us, event | category | flops | bytes accessed | tf_op | source)
XLA Modules:
  0.0 1515.2 jit_solution(16040654577957878719)
XLA Ops:
  7.3 2.1 fusion.17
  9.9 2.9 multiply_reduce_fusion.6
  17.2 1.6 constant_dynamic-slice_fusion.1
  18.9 1.6 constant_dynamic-slice_fusion
  23.7 17.6 %all-gather.12.cloned.1.call-done = bf16[1024,512]{0,1:T(8,128)(2,1)} async-done(((bf16[512,512]{0,1:T(8,128)(2,1)}), bf16[1024,512]{0,1:T(8,128)(2,1)}) %all-gather.12.cloned.1.call-update) | async-done | bytes 1048592 | tf_op jit(solution)/shard_map/all_gather | solution.py:148
  41.3 2.2 fusion.72
  43.6 63.4 %all-gather.22.cloned.1.call-done = bf16[8192,256]{1,0:T(8,128)(2,1)} async-done(((bf16[256,256]{1,0:T(8,128)(2,1)}), bf16[8192,256]{1,0:T(8,128)(2,1)}) %all-gather.22.cloned.1.call-update) | async-done | bytes 4194320 | tf_op jit(solution)/shard_map/all_gather | solution.py:132
  107.0 8.3 copy.56
  115.3 3.7 copy.73
  119.1 2.5 multiply_reduce_fusion.4
  123.9 13.6 fusion.9
  137.5 14.9 fusion.3
  153.1 16.4 %fusion.33 = bf16[4,64,4,512]{3,1,2,0:T(8,128)(2,1)} fusion(bf16[1024,4,64,1]{0,2,3,1:T(8,128)(2,1)S(1)} %bitcast.229, f32[4,4,512]{2,1,0:T(4,128)S(1)} %fusion.3, f32[4,4,512]{2,1,0:T(4,128)S(1)} %get-tuple-element.123, pred[512,1024]{0,1:T(8,128)(4,1)S(1)} %copy-done.10, f32[4,1024,512,4]{2,1,3,0:T(8,128)} %get-tuple-element.124), kind=kOutput, calls=%fused_computation.80 | convolution fusion | flops 1124597760 | bytes 35717120 | tf_op jit(solution)/shard_map/kgij,jkd->ikgd/dot_general | solution.py:76
  169.5 1.5 all-gather.14.cloned.1.call-done
  171.1 5.2 multiply_reduce_fusion.1
  178.3 1.7 multiply_convert_fusion.3
  180.1 148.3 %all-gather.16.cloned.1.call-done = bf16[2048,2048]{1,0:T(8,128)(2,1)} async-done(((bf16[512,2048]{1,0:T(8,128)(2,1)}), bf16[2048,2048]{1,0:T(8,128)(2,1)}) %all-gather.16.cloned.1.call-update) | async-done | bytes 8388624 | tf_op jit(solution)/shard_map/all_gather | solution.py:165
  328.4 16.7 %fusion.78 = f32[2048,1280]{1,0:T(8,128)} fusion(bf16[2048,2048]{1,0:T(8,128)(2,1)} %all-gather.16.cloned.1.call-done, bf16[2048,1280]{1,0:T(8,128)(2,1)} %param.27), kind=kOutput, calls=%fused_computation.162 | convolution fusion | flops 10737418240 | bytes 24117248 | tf_op jit(solution)/shard_map/dot_general | solution.py:47
  345.0 17.3 %multiply_convert_fusion.2 = (bf16[2048,1280]{1,0:T(8,128)(2,1)}, f32[2048,1280]{1,0:T(8,128)}) fusion(f32[2048,1280]{1,0:T(8,128)} %fusion.78, bf16[2048,2048]{1,0:T(8,128)(2,1)S(1)} %copy-done.77, bf16[2048,1280]{1,0:T(8,128)(2,1)} %param.28), kind=kOutput, calls=%fused_computation.19 | convolution fusion | flops 10753146880 | bytes 39845888 | tf_op jit(solution)/shard_map/dot_general | solution.py:47
  362.3 16.6 %convolution_convert_fusion = bf16[2048,2048]{1,0:T(8,128)(2,1)} fusion(bf16[2048,1280]{1,0:T(8,128)(2,1)} %get-tuple-element.127, bf16[1280,2048]{1,0:T(8,128)(2,1)} %param.29), kind=kOutput, calls=%fused_computation.27 | convolution fusion | flops 10741612544 | bytes 18874368 | tf_op jit(solution)/shard_map/dot_general | solution.py:47
  381.0 42.9 %all-reduce = f32[32]{0:T(128)S(1)} all-reduce(f32[32]{0:T(128)S(1)} %dynamic-update-slice), channel_id=2, replica_groups=mesh['dp'=8,'tensor'=4] {'dp','tensor'}, use_global_device_ids=true, to_apply=%add | all-reduce | flops 32 | bytes 256
  424.1 98.7 %reduce-scatter.6.cloned.1.call-done = bf16[512,2048]{1,0:T(8,128)(2,1)} async-done(((bf16[2048,2048]{1,0:T(8,128)(2,1)}), bf16[512,2048]{1,0:T(8,128)(2,1)}) %reduce-scatter.6.cloned.1.call-update) | async-done | bytes 2097168 | tf_op jit(solution)/shard_map/reduce_scatter | solution.py:170
  522.8 5.4 fusion.26
  528.2 150.4 %all-gather.18.cloned.1.call-done = bf16[2048,2048]{1,0:T(8,128)(2,1)} async-done(((bf16[512,2048]{1,0:T(8,128)(2,1)}), bf16[2048,2048]{1,0:T(8,128)(2,1)}) %all-gather.18.cloned.1.call-update) | async-done | bytes 8388624 | tf_op jit(solution)/shard_map/all_gather | solution.py:177
  678.7 24.3 %multiply_convert_fusion = (bf16[2048,1280]{1,0:T(8,128)(2,1)}, bf16[2048,1280]{1,0:T(8,128)(2,1)}) fusion(f32[2048,1280]{1,0:T(8,128)} %fusion.78, f32[2048,1280]{1,0:T(8,128)} %get-tuple-element.128, bf16[2048,2048]{1,0:T(8,128)(2,1)} %all-gather.18.cloned.1.call-done, bf16[1280,2048]{1,0:T(8,128)(2,1)} %param.29), kind=kOutput, calls=%fused_computation.17 | convolution fusion | flops 10771496960 | bytes 45088768 | tf_op jit(solution)/shard_map/dot_general | solution.py:51
  702.9 17.9 %fusion.79 = f32[2048,2048]{1,0:T(8,128)} fusion(bf16[2048,1280]{1,0:T(8,128)(2,1)} %get-tuple-element.82, bf16[2048,1280]{1,0:T(8,128)(2,1)} %param.27), kind=kOutput, calls=%fused_computation.163 | convolution fusion | flops 10737418240 | bytes 27262976 | tf_op jit(solution)/shard_map/dot_general | solution.py:51
  720.8 19.2 %add_convert_fusion = bf16[2048,2048]{1,0:T(8,128)(2,1)} fusion(f32[2048,2048]{1,0:T(8,128)} %fusion.79, bf16[2048,1280]{1,0:T(8,128)(2,1)} %get-tuple-element.81, bf16[2048,1280]{1,0:T(8,128)(2,1)} %param.28), kind=kOutput, calls=%fused_computation.11 | convolution fusion | flops 10745806848 | bytes 35651584 | tf_op jit(solution)/shard_map/dot_general | solution.py:51
  740.8 142.1 %reduce-scatter.8.cloned.1.call-done = bf16[512,2048]{1,0:T(8,128)(2,1)} async-done(((bf16[2048,2048]{1,0:T(8,128)(2,1)}), bf16[512,2048]{1,0:T(8,128)(2,1)}) %reduce-scatter.8.cloned.1.call-update) | async-done | bytes 2097168 | tf_op jit(solution)/shard_map/reduce_scatter | solution.py:182
  883.0 6.4 fusion.16
  889.3 3.5 fusion.13
  892.9 1.9 copy-done.16
  894.8 3.3 convolution_convert_fusion.7
  899.7 24.3 %fusion = (f32[4,4,512]{2,1,0:T(4,128)S(1)}, f32[4,1024,512,4]{2,1,3,0:T(8,128)}) fusion(f32[4,4,512]{2,1,0:T(4,128)S(1)} %bitcast.233, pred[512,1024]{0,1:T(8,128)(4,1)S(1)} %copy-done.11, f32[4,1024,512,4]{2,1,3,0:T(8,128)} %get-tuple-element.124, bf16[1024,4,64,1]{0,2,3,1:T(8,128)(2,1)S(1)} %bitcast.230, bf16[512,4,4,64]{0,3,2,1:T(8,128)(2,1)S(1)} %bitcast.227), kind=kOutput, calls=%fused_computation.2 | convolution fusion | flops 1124065280 | bytes 69271552 | tf_op jit(solution)/shard_map/ikgd,jkd->kgij/dot_general | solution.py:88
  924.0 16.1 %fusion.39 = bf16[4,64,1024]{2,1,0:T(8,128)(2,1)} fusion(bf16[512,4,4,64]{0,3,2,1:T(8,128)(2,1)S(1)} %bitcast.228, f32[4,4,512]{2,1,0:T(4,128)S(1)} %bitcast.234, pred[512,1024]{0,1:T(8,128)(4,1)S(1)} %copy-done.11, f32[4,1024,512,4]{2,1,3,0:T(8,128)} %get-tuple-element.124), kind=kOutput, calls=%fused_computation.86 | convolution fusion | flops 1115947008 | bytes 35684352 | tf_op jit(solution)/shard_map/kgij,ikgd->jkd/dot_general | solution.py:93
  940.2 28.0 %fusion.2 = bf16[4,4,512,1024]{2,3,1,0:T(8,128)(2,1)} fusion(f32[4,1024,512,4]{2,1,3,0:T(8,128)} %get-tuple-element.130, f32[4,4,512]{2,1,0:T(4,128)S(1)} %get-tuple-element.129, f32[4,4,512]{2,1,0:T(4,128)S(1)} %bitcast.235, pred[512,1024]{0,1:T(8,128)(4,1)S(1)} %copy-done.11, f32[4,1024,512,4]{2,1,3,0:T(8,128)} %get-tuple-element.124), kind=kLoop, calls=%fused_computation.4 | loop fusion | flops 58720256 | bytes 84475904 | tf_op jit(solution)/shard_map/convert_element_type | solution.py:90
  968.2 11.0 fusion.38
  979.2 10.1 convolution_multiply_fusion
  990.6 2.0 bitcast_multiply_fusion.1
  993.4 1.5 multiply_reduce_fusion.2
  996.5 4.5 convolution_convert_fusion.5
  1001.0 4.4 convolution_convert_fusion.4
  1005.4 6.3 reduce-scatter.10.cloned.1.call-done
  1018.6 18.0 %pad_maximum_fusion = bf16[2048,2560]{0,1:T(8,128)(2,1)} fusion(bf16[2048,512]{0,1:T(8,128)(2,1)S(1)} %convolution_convert_fusion.6, bf16[2048,1024]{0,1:T(8,128)(2,1)S(1)} %copy-done.34, bf16[2048,1024]{0,1:T(8,128)(2,1)S(1)} %copy-done.33), kind=kLoop, calls=%fused_computation.16 | loop fusion | flops 31457280 | bytes 20971520 | tf_op jit(solution)/shard_map/concatenate | solution.py:220
  1036.8 16.7 %convolution_convert_fusion.2 = bf16[2048,1280]{1,0:T(8,128)(2,1)} fusion(bf16[2048,2048]{1,0:T(8,128)(2,1)} %all-gather.16.cloned.1.call-done, bf16[2048,1280]{1,0:T(8,128)(2,1)} %get-tuple-element.81), kind=kOutput, calls=%fused_computation.29 | convolution fusion | flops 10740039680 | bytes 18874368 | tf_op jit(solution)/shard_map/dot_general | solution.py:55
  1053.5 17.0 %convolution_convert_fusion.3 = bf16[2048,1280]{1,0:T(8,128)(2,1)} fusion(bf16[2048,2048]{1,0:T(8,128)(2,1)} %all-gather.16.cloned.1.call-done, bf16[2048,1280]{1,0:T(8,128)(2,1)} %get-tuple-element.82), kind=kOutput, calls=%fused_computation.30 | convolution fusion | flops 10740039680 | bytes 18874368 | tf_op jit(solution)/shard_map/dot_general | solution.py:55
  1070.5 47.8 %reduce-scatter.12.cloned.1.call-done = bf16[256,2560]{0,1:T(8,128)(2,1)} async-done(((bf16[2048,2560]{0,1:T(8,128)(2,1)}), bf16[256,2560]{0,1:T(8,128)(2,1)}) %reduce-scatter.12.cloned.1.call-update) | async-done | bytes 1310736 | tf_op jit(solution)/shard_map/reduce_scatter | solution.py:221
  1121.2 16.6 %convolution_convert_fusion.1 = bf16[1280,2048]{1,0:T(8,128)(2,1)} fusion(bf16[2048,1280]{1,0:T(8,128)(2,1)} %get-tuple-element.127, bf16[2048,2048]{1,0:T(8,128)(2,1)} %all-gather.18.cloned.1.call-done), kind=kOutput, calls=%fused_computation.28 | convolution fusion | flops 10740039680 | bytes 18874368 | tf_op jit(solution)/shard_map/dot_general | solution.py:55
  1137.8 14.5 reduce-scatter.14.cloned.1.call-done
  1152.4 1.7 slice.124
  1155.7 208.1 %all-reduce.4.cloned.1.call-done = (bf16[2048,1280]{1,0:T(8,128)(2,1)}, bf16[2048,1280]{1,0:T(8,128)(2,1)}, bf16[1280,2048]{1,0:T(8,128)(2,1)}) async-done(((bf16[2048,1280]{1,0:T(8,128)(2,1)}, bf16[2048,1280]{1,0:T(8,128)(2,1)}, bf16[1280,2048]{1,0:T(8,128)(2,1)}), (bf16[2048,1280]{1,0:T(8,128)(2,1)}, bf16[2048,1280]{1,0:T(8,128)(2,1)}, bf16[1280,2048]{1,0:T(8,128)(2,1)})) %all-reduce.4.cloned.1.call-update) | async-done | bytes 15728656 | tf_op jit(solution)/shard_map/psum | solution.py:191
  1363.7 7.9 convert_element_type.180
  1371.7 4.9 convert_element_type.182
  1376.6 5.5 convert_element_type.184
  1382.1 4.4 fusion.80
  1386.6 2.1 fusion.81
  1389.2 3.7 fusion.25
  1393.7 78.0 %all-gather.3 = f32[32,1,4352]{2,1,0:T(1,128)} all-gather(f32[1,1,4352]{2,1,0:T(1,128)S(1)} %reshape.250), channel_id=4, replica_groups=mesh['dp'=8,'tensor'=4] {'dp','tensor'}, dimensions={0}, use_global_device_ids=true | all-gather | bytes 574464 | tf_op jit(solution)/shard_map/all_gather | solution.py:98
  1475.4 6.6 fusion.24
  1482.0 2.9 slice.125
  1485.0 2.9 copy.64
  1489.8 6.0 reshape.239
  1495.9 6.5 copy.63
  1502.4 2.6 copy.76
  1505.0 2.3 fusion.70
  (254 shorter events, 38.3 us)
Async XLA Ops:
  7.2 7.5 copy-start
  7.2 6.5 copy-start.72
  7.2 34.1 %all-gather.12.cloned.1.call-start = ((), (), s32[]{:S(2)}) async-start(), calls=%async_computation.5 | async-start | bytes 1572864 | tf_op jit(solution)/shard_map/all_gather | solution.py:148
  9.4 5.3 copy-start.5
  9.4 5.3 copy-start.56
  9.9 109.1 %copy-start.62 = (f32[512]{0:T(512)}, f32[512]{0:T(512)S(1)}, u32[]{:S(2)}) copy-start(f32[512]{0:T(512)S(1)} %get-tuple-element.114) | copy-start | bytes 6148
  14.7 5.8 copy-start.78
  16.0 107.0 %copy-start.30 = (f32[512,64]{0,1:T(8,128)}, f32[512,64]{0,1:T(8,128)S(1)}, u32[]{:S(2)}) copy-start(f32[512,64]{0,1:T(8,128)S(1)} %get-tuple-element.132) | copy-start | bytes 393220
  16.0 107.0 %copy-start.35 = (f32[512,64]{0,1:T(8,128)}, f32[512,64]{0,1:T(8,128)S(1)}, u32[]{:S(2)}) copy-start(f32[512,64]{0,1:T(8,128)S(1)} %get-tuple-element.133) | copy-start | bytes 393220
  17.1 89.8 %all-gather.22.cloned.1.call-start = ((), (), s32[]{:S(2)}) async-start(), calls=%async_computation.15 | async-start | bytes 4325376 | tf_op jit(solution)/shard_map/all_gather | solution.py:132
  18.8 152.3 %all-gather.14.cloned.1.call-start = ((), (), s32[]{:S(2)}) async-start(), calls=%async_computation.6 | async-start | bytes 4325376 | tf_op jit(solution)/shard_map/all_gather | solution.py:139
  20.4 307.9 %all-gather.16.cloned.1.call-start = ((), (), s32[]{:S(2)}) async-start(), calls=%async_computation.7 | async-start | bytes 10485760 | tf_op jit(solution)/shard_map/all_gather | solution.py:165
  119.0 3.2 copy-start.68
  123.8 13.7 copy-start.18
  137.5 15.0 copy-start.47
  137.5 15.6 %copy-start.44 = (bf16[1024,256]{0,1:T(8,128)(2,1)S(1)}, bf16[1024,256]{0,1:T(8,128)(2,1)}, u32[]{:S(2)}) copy-start(bf16[1024,256]{0,1:T(8,128)(2,1)} %get-tuple-element.94) | copy-start | bytes 1572868
  171.1 7.2 copy-start.54
  180.0 342.7 %reduce-scatter.6.cloned.1.call-start = ((), (), s32[]{:S(2)}) async-start(), calls=%async_computation.8 | async-start | bytes 10485760 | tf_op jit(solution)/shard_map/reduce_scatter | solution.py:170
  328.4 16.7 %copy-start.77 = (bf16[2048,2048]{1,0:T(8,128)(2,1)S(1)}, bf16[2048,2048]{1,0:T(8,128)(2,1)}, u32[]{:S(2)}) copy-start(bf16[2048,2048]{1,0:T(8,128)(2,1)} %all-gather.16.cloned.1.call-done) | copy-start | bytes 25165828
  378.9 143.9 %copy-start.13 = (bf16[512,2048]{1,0:T(8,128)(2,1)S(1)}, bf16[512,2048]{1,0:T(8,128)(2,1)}, u32[]{:S(2)}) copy-start(bf16[512,2048]{1,0:T(8,128)(2,1)} %param.16) | copy-start | bytes 6291460
  378.9 299.8 %all-gather.18.cloned.1.call-start = ((), (), s32[]{:S(2)}) async-start(), calls=%async_computation.9 | async-start | bytes 10485760 | tf_op jit(solution)/shard_map/all_gather | solution.py:177
  424.0 104.2 %copy-start.79 = (f32[128]{0:T(128)}, f32[128]{0:T(128)S(1)}, u32[]{:S(2)}) copy-start(f32[128]{0:T(128)S(1)} %broadcast_reduce_fusion) | copy-start | bytes 1540
  528.2 354.7 %reduce-scatter.8.cloned.1.call-start = ((), (), s32[]{:S(2)}) async-start(), calls=%async_computation.10 | async-start | bytes 10485760 | tf_op jit(solution)/shard_map/reduce_scatter | solution.py:182
  740.0 142.9 %copy-start.55 = (f32[2048]{0:T(1024)S(1)}, f32[2048]{0:T(1024)}, u32[]{:S(2)}) copy-start(f32[2048]{0:T(1024)} %param.26) | copy-start | bytes 24580
  740.0 142.9 %copy-start.61 = (f32[512]{0:T(512)S(1)}, f32[512]{0:T(512)}, u32[]{:S(2)}) copy-start(f32[512]{0:T(512)} %copy-done.60) | copy-start | bytes 6148
  740.1 271.6 %reduce-scatter.10.cloned.1.call-start = ((), (), s32[]{:S(2)}) async-start(), calls=%async_computation.11 | async-start | bytes 1572864 | tf_op jit(solution)/shard_map/reduce_scatter | solution.py:199
  740.8 148.5 %copy-start.71 = (f32[512]{0:T(512)S(1)}, f32[512]{0:T(512)}, u32[]{:S(2)}) copy-start(f32[512]{0:T(512)} %get-tuple-element.115) | copy-start | bytes 6148
  882.9 6.4 copy-start.2
  882.9 6.4 copy-start.14
  882.9 6.4 copy-start.24
  889.3 5.5 copy-start.32
  894.8 4.8 copy-start.11
  894.8 4.9 copy-start.45
  940.2 28.1 %copy-start.19 = (bf16[512,16,64]{0,2,1:T(8,128)(2,1)S(1)}, bf16[512,16,64]{0,2,1:T(8,128)(2,1)}, u32[]{:S(2)}) copy-start(bf16[512,16,64]{0,2,1:T(8,128)(2,1)} %copy-done.18) | copy-start | bytes 3145732
  968.2 11.0 copy-start.29
  979.2 10.2 copy-start.46
  979.2 11.3 copy-start.36
  990.5 127.8 %reduce-scatter.12.cloned.1.call-start = ((), (), s32[]{:S(2)}) async-start(), calls=%async_computation.12 | async-start | bytes 11796480 | tf_op jit(solution)/shard_map/reduce_scatter | solution.py:221
  990.5 2.8 copy-start.12
  995.7 5.3 copy-start.25
  996.5 4.5 copy-start.17
  996.5 4.5 copy-start.39
  1001.0 11.9 copy-start.73
  1005.4 8.9 copy-start.50
  1005.4 9.8 copy-start.7
  1011.7 2.7 copy-start.58
  1011.7 2.7 copy-start.67
  1011.7 3.5 copy-start.64
  1015.1 3.5 copy-start.34
  1036.6 115.8 %reduce-scatter.14.cloned.1.call-start = ((), (), s32[]{:S(2)}) async-start(), calls=%async_computation.13 | async-start | bytes 1638400 | tf_op jit(solution)/shard_map/reduce_scatter | solution.py:232
  1120.9 242.8 %all-reduce.4.cloned.1.call-start = ((), (), s32[]{:S(2)}) async-start(), calls=%async_computation.17 | async-start | bytes 31457280 | tf_op jit(solution)/shard_map/psum | solution.py:191
  1137.8 17.9 %copy-start.80 = (f32[128]{0:T(128)S(1)}, f32[128]{0:T(128)}, u32[]{:S(2)}) copy-start(f32[128]{0:T(128)} %copy-done.79) | copy-start | bytes 1540
  1137.8 344.2 %all-gather.20.cloned.1.call-start = ((), (), s32[]{:S(2)}) async-start(), calls=%async_computation.14 | async-start | bytes 2359296 | tf_op jit(solution)/shard_map/all_gather | solution.py:233
  1154.1 335.8 %all-gather.24.cloned.1.call-start = ((), (), s32[]{:S(2)}) async-start(), calls=%async_computation.16 | async-start | bytes 2162688 | tf_op jit(solution)/shard_map/all_gather | solution.py:237
  1363.7 8.0 copy-start.27
  1363.7 12.9 slice-start
  1371.7 4.9 slice-start.1
  1376.6 5.5 copy-start.9
  1376.6 5.5 copy-start.26
  1382.1 4.4 copy-start.74
  1389.2 4.3 copy-start.59
  1389.2 4.3 copy-start.75
  1389.2 86.2 %copy-start.70 = (f32[512]{0:T(512)S(1)}, f32[512]{0:T(512)}, u32[]{:S(2)}) copy-start(f32[512]{0:T(512)} %get-tuple-element.113) | copy-start | bytes 6148
  1482.0 5.8 copy-start.20
  (33 other events, 57.1 us)
Sparse Core Ops, SparseCore 0:
  17.3 23.9 all-gather.11
  44.9 62.0 all-gather.21
  110.4 60.5 all-gather.13
  180.1 148.1 all-gather.15
  379.0 143.7 reduce-scatter.5
  528.3 150.2 all-gather.17
  740.2 142.6 reduce-scatter.7
  990.6 21.0 reduce-scatter.9
  1036.7 81.5 reduce-scatter.11
  1121.1 31.1 reduce-scatter.13
  1157.4 206.2 all-reduce.3
  1366.0 28.3 all-gather.19
  1397.8 58.5 all-gather.23
where the time goes:
time: 1520 us
  waiting for transfers between devices  899 us (59%)
  matrix products  289 us (19%)
  other arithmetic  127 us (8%)
  blocking collectives  121 us (8%)
  local copies, waits for them, and re-layouts  61 us (4%)
  between operations  17.7 us (1%)
    psum x1, waiting for transfers between devices, body(): lax.psum(g.astype(BF), 'dp').astype(F32)  208 us
    all_gather x1, waiting for transfers between devices, body(): cot_all = lax.all_gather(cot.astype(BF), 'tensor', axis=0, tiled=True)  150 us
    all_gather x1, waiting for transfers between devices, body(): normed_two_all = lax.all_gather(normed_two, 'tensor', axis=0, tiled=True)  148 us
    reduce_scatter x1, waiting for transfers between devices, body(): lax.psum_scatter((dot_t(dgate, w_gate) + dot_t(dup, w_up)).astype(BF), 't...  142 us
    reduce_scatter x1, waiting for transfers between devices, body(): lax.psum_scatter(dot(hidden, w_down).astype(BF), 'tensor', scatter_dimens...  98.7 us
    all_gather x1, blocking collectives, sum_small(): lax.all_gather(vector[None], ('dp', 'tensor'), axis=0, tiled=True)  78 us
    dot_general x7, matrix products, dot_t(): lax.dot_general(a, b, (((1,), (1,)), ((), ())), preferred_element_type=F32)  74.9 us
    all_gather x1, waiting for transfers between devices, body(): lax.all_gather(query_cut, ('dp', 'tensor'), axis=0, tiled=False)  63.4 us
  transfers between devices with their start and end apart: 13, of which 11 were waited for; matrix products, arithmetic and copies ran while one was open for 12% of the time, Pallas kernels for 0%

commit v1 on v0

--- a/solution.py
+++ b/solution.py
@@ -11,6 +11,11 @@
 EPSILON = 1e-06
 BF = jnp.bfloat16
 F32 = jnp.float32
+
+
+def gather_and_add(block, axis):
+    parts = lax.all_gather(block, axis)
+    return jnp.sum(parts, axis=0)
 
 
 def rope_rows(start, rows):
@@ -188,7 +193,7 @@
     grad_gate = t_dot(normed_two_all, dgate)
     grad_up = t_dot(normed_two_all, dup)
     grad_gate, grad_up, grad_down = (
-        lax.psum(g.astype(BF), "dp").astype(F32) for g in (grad_gate, grad_up, grad_down)
+        gather_and_add(g.astype(BF), "dp").astype(F32) for g in (grad_gate, grad_up, grad_down)
     )
     grad_ffn_gain = jnp.sum(dn2 * middle * factor_two, 0)
     dmiddle = cot + norm_back(dn2, middle, factor_two, ffn_gain)

time: 1520 us -> 1880 us (1.24)
  waiting for transfers between devices: 899 us -> 1190 us
  other arithmetic: 127 us -> 194 us
    all_gather x0 -> x3, waiting for transfers between devices: none -> 449 us  [gather_and_add(): parts = lax.all_gather(block, axis)]
    psum x1 -> x0, waiting for transfers between devices: 208 us -> none  [body(): lax.psum(g.astype(BF), 'dp').astype(F32)]
    reduce_sum x0 -> x3, other arithmetic: none -> 59.7 us  [gather_and_add(): return jnp.sum(parts, axis=0)]
    reduce_scatter x1, waiting for transfers between devices: 47.8 us -> 81.7 us  [body(): wide = lax.psum_scatter(wide, 'dp', scatter_dimension=0, tiled=True)]
  transfers between devices with their start and end apart: 13 -> 15, of which waited for: 11 -> 13; matrix products, arithmetic and copies ran while one was open for 12% -> 13% of each run, Pallas kernels for 0% -> 0%
where the time goes in v1:
time: 1880 us
  waiting for transfers between devices  1190 us (63%)
  matrix products  292 us (16%)
  other arithmetic  194 us (10%)
  blocking collectives  121 us (6%)
  local copies, waits for them, and re-layouts  63 us (3%)
    all_gather x3, waiting for transfers between devices, gather_and_add(): parts = lax.all_gather(block, axis)  449 us
    all_gather x1, waiting for transfers between devices, body(): cot_all = lax.all_gather(cot.astype(BF), 'tensor', axis=0, tiled=True)  150 us
    all_gather x1, waiting for transfers between devices, body(): normed_two_all = lax.all_gather(normed_two, 'tensor', axis=0, tiled=True)  148 us
    reduce_scatter x1, waiting for transfers between devices, body(): lax.psum_scatter((dot_t(dgate, w_gate) + dot_t(dup, w_up)).astype(BF), 't...  142 us
    reduce_scatter x1, waiting for transfers between devices, body(): lax.psum_scatter(dot(hidden, w_down).astype(BF), 'tensor', scatter_dimens...  98.6 us
    reduce_scatter x1, waiting for transfers between devices, body(): wide = lax.psum_scatter(wide, 'dp', scatter_dimension=0, tiled=True)  81.7 us
    all_gather x1, blocking collectives, sum_small(): lax.all_gather(vector[None], ('dp', 'tensor'), axis=0, tiled=True)  78 us
    dot_general x7, matrix products, dot_t(): lax.dot_general(a, b, (((1,), (1,)), ((), ())), preferred_element_type=F32)  77.5 us
  transfers between devices with their start and end apart: 15, of which 13 were waited for; matrix products, arithmetic and copies ran while one was open for 13% of the time, Pallas kernels for 0%

profile of v1, /device:TPU:0, one launch (start us, length us, event | category | flops | bytes accessed | tf_op | source)
XLA Modules:
  0.0 1879.7 jit_solution(5902942262046025155)
XLA Ops:
  7.3 2.2 fusion.17
  10.1 3.2 convolution_convert_fusion.8
  18.9 1.8 pad_maximum_fusion.3
  27.3 17.6 all-gather.18.cloned.1.call-done
  44.9 2.2 fusion.72
  47.2 63.4 %all-gather.28.cloned.1.call-done = bf16[8192,256]{1,0:T(8,128)(2,1)} async-done(((bf16[256,256]{1,0:T(8,128)(2,1)}), bf16[8192,256]{1,0:T(8,128)(2,1)}) %all-gather.28.cloned.1.call-update) | async-done | bytes 4194320 | tf_op jit(solution)/shard_map/all_gather | solution.py:137
  110.6 8.0 copy.56
  118.6 3.7 copy.73
  122.3 2.5 multiply_reduce_fusion.4
  127.2 13.6 fusion.9
  140.8 14.9 fusion.3
  156.3 16.6 fusion.33
  174.7 5.2 multiply_reduce_fusion.1
  183.7 148.3 %all-gather.22.cloned.1.call-done = bf16[2048,2048]{1,0:T(8,128)(2,1)} async-done(((bf16[512,2048]{1,0:T(8,128)(2,1)}), bf16[2048,2048]{1,0:T(8,128)(2,1)}) %all-gather.22.cloned.1.call-update) | async-done | bytes 8388624 | tf_op jit(solution)/shard_map/all_gather | solution.py:170
  332.0 16.7 fusion.78
  348.7 17.3 multiply_convert_fusion.2
  365.9 16.5 convolution_convert_fusion
  384.6 43.0 %all-reduce = f32[32]{0:T(128)S(1)} all-reduce(f32[32]{0:T(128)S(1)} %dynamic-update-slice), channel_id=2, replica_groups=mesh['dp'=8,'tensor'=4] {'dp','tensor'}, use_global_device_ids=true, to_apply=%add | all-reduce | flops 32 | bytes 256
  427.7 98.6 %reduce-scatter.6.cloned.1.call-done = bf16[512,2048]{1,0:T(8,128)(2,1)} async-done(((bf16[2048,2048]{1,0:T(8,128)(2,1)}), bf16[512,2048]{1,0:T(8,128)(2,1)}) %reduce-scatter.6.cloned.1.call-update) | async-done | bytes 2097168 | tf_op jit(solution)/shard_map/reduce_scatter | solution.py:175
  526.4 5.4 fusion.26
  531.9 150.5 %all-gather.24.cloned.1.call-done = bf16[2048,2048]{1,0:T(8,128)(2,1)} async-done(((bf16[512,2048]{1,0:T(8,128)(2,1)}), bf16[2048,2048]{1,0:T(8,128)(2,1)}) %all-gather.24.cloned.1.call-update) | async-done | bytes 8388624 | tf_op jit(solution)/shard_map/all_gather | solution.py:182
  682.3 24.3 %multiply_convert_fusion = (bf16[2048,1280]{1,0:T(8,128)(2,1)}, bf16[2048,1280]{1,0:T(8,128)(2,1)}) fusion(f32[2048,1280]{1,0:T(8,128)} %fusion.78, f32[2048,1280]{1,0:T(8,128)} %get-tuple-element.125, bf16[2048,2048]{1,0:T(8,128)(2,1)} %all-gather.24.cloned.1.call-done, bf16[1280,2048]{1,0:T(8,128)(2,1)} %param.29), kind=kOutput, calls=%fused_computation.17 | convolution fusion | flops 10771496960 | bytes 45088768 | tf_op jit(solution)/shard_map/dot_general | solution.py:56
  706.6 17.8 fusion.79
  724.4 19.4 %add_convert_fusion = bf16[2048,2048]{1,0:T(8,128)(2,1)} fusion(f32[2048,2048]{1,0:T(8,128)} %fusion.79, bf16[2048,1280]{1,0:T(8,128)(2,1)} %get-tuple-element.78, bf16[2048,1280]{1,0:T(8,128)(2,1)} %param.28), kind=kOutput, calls=%fused_computation.11 | convolution fusion | flops 10745806848 | bytes 35651584 | tf_op jit(solution)/shard_map/dot_general | solution.py:56
  744.6 142.1 %reduce-scatter.8.cloned.1.call-done = bf16[512,2048]{1,0:T(8,128)(2,1)} async-done(((bf16[2048,2048]{1,0:T(8,128)(2,1)}), bf16[512,2048]{1,0:T(8,128)(2,1)}) %reduce-scatter.8.cloned.1.call-update) | async-done | bytes 2097168 | tf_op jit(solution)/shard_map/reduce_scatter | solution.py:187
  886.7 6.5 fusion.16
  893.3 3.5 fusion.13
  896.8 2.0 copy-done.15
  898.8 3.3 convolution_convert_fusion.7
  903.7 15.8 fusion.39
  919.5 24.5 %fusion = (f32[4,4,512]{2,1,0:T(4,128)S(1)}, f32[4,1024,512,4]{2,1,3,0:T(8,128)}) fusion(f32[4,4,512]{2,1,0:T(4,128)S(1)} %bitcast.238, pred[512,1024]{0,1:T(8,128)(4,1)S(1)} %copy-done.10, f32[4,1024,512,4]{2,1,3,0:T(8,128)} %get-tuple-element.121, bf16[1024,4,64,1]{0,2,3,1:T(8,128)(2,1)S(1)} %bitcast.234, bf16[512,4,4,64]{0,3,2,1:T(8,128)(2,1)S(1)} %bitcast.232), kind=kOutput, calls=%fused_computation.2 | convolution fusion | flops 1124065280 | bytes 69271552 | tf_op jit(solution)/shard_map/ikgd,jkd->kgij/dot_general | solution.py:93
  944.0 28.1 %fusion.2 = bf16[4,4,512,1024]{2,3,1,0:T(8,128)(2,1)} fusion(f32[4,1024,512,4]{2,1,3,0:T(8,128)} %get-tuple-element.127, f32[4,4,512]{2,1,0:T(4,128)S(1)} %get-tuple-element.126, f32[4,4,512]{2,1,0:T(4,128)S(1)} %bitcast.239, pred[512,1024]{0,1:T(8,128)(4,1)S(1)} %copy-done.10, f32[4,1024,512,4]{2,1,3,0:T(8,128)} %get-tuple-element.121), kind=kLoop, calls=%fused_computation.4 | loop fusion | flops 58720256 | bytes 84475904 | tf_op jit(solution)/shard_map/convert_element_type | solution.py:95
  972.2 11.0 fusion.38
  983.1 10.1 convolution_multiply_fusion
  994.5 2.0 bitcast_multiply_fusion.1
  1000.4 4.5 convolution_convert_fusion.5
  1004.9 4.4 convolution_convert_fusion.4
  1009.3 6.3 reduce-scatter.10.cloned.1.call-done
  1022.5 18.0 pad_maximum_fusion
  1040.6 81.7 %reduce-scatter.12.cloned.1.call-done = bf16[256,2560]{0,1:T(8,128)(2,1)} async-done(((bf16[2048,2560]{0,1:T(8,128)(2,1)}), bf16[256,2560]{0,1:T(8,128)(2,1)}) %reduce-scatter.12.cloned.1.call-update) | async-done | bytes 1310736 | tf_op jit(solution)/shard_map/reduce_scatter | solution.py:226
  1124.9 31.4 %reduce-scatter.14.cloned.1.call-done = bf16[256,640]{0,1:T(8,128)(2,1)} async-done(((bf16[256,2560]{0,1:T(8,128)(2,1)}), bf16[256,640]{0,1:T(8,128)(2,1)}) %reduce-scatter.14.cloned.1.call-update) | async-done | bytes 327696 | tf_op jit(solution)/shard_map/reduce_scatter | solution.py:237
  1160.0 16.7 convolution_convert_fusion.3
  1176.8 16.7 convolution_convert_fusion.2
  1193.8 16.7 convolution_convert_fusion.1
  1211.2 6.9 fusion.80
  1218.2 2.1 fusion.81
  1220.8 3.7 fusion.25
  1225.3 78.0 %all-gather.6 = f32[32,1,4352]{2,1,0:T(1,128)} all-gather(f32[1,1,4352]{2,1,0:T(1,128)S(1)} %reshape.253), channel_id=4, replica_groups=mesh['dp'=8,'tensor'=4] {'dp','tensor'}, dimensions={0}, use_global_device_ids=true | all-gather | bytes 574464 | tf_op jit(solution)/shard_map/all_gather | solution.py:103
  1307.0 6.6 fusion.24
  1313.6 2.9 slice.125
  1316.5 2.9 copy.64
  1321.4 6.0 reshape.239
  1327.4 6.8 copy.63
  1334.2 3.9 copy.76
  1338.1 2.3 fusion.70
  1340.5 107.4 %all-gather.32.cloned.1.call-done = bf16[16384,1280]{1,0:T(8,128)(2,1)} async-done(((bf16[2048,1280]{1,0:T(8,128)(2,1)}), bf16[16384,1280]{1,0:T(8,128)(2,1)}) %all-gather.32.cloned.1.call-update) | async-done | bytes 41943056 | tf_op jit(solution)/shard_map/all_gather | solution.py:17
  1447.9 21.1 %reduce_sum.225 = bf16[2048,1280]{1,0:T(8,128)(2,1)} reduce(bf16[8,2048,1280]{2,1,0:T(8,128)(2,1)} %bitcast.207, bf16[]{:T(256)} %constant.87.clone.1), dimensions={0}, to_apply=%region_25.26 | reduce | flops 18350080 | bytes 47185920 | tf_op jit(solution)/shard_map/reduce_sum | solution.py:18
  1468.9 7.4 convert_element_type.186
  1476.3 171.2 %all-gather.34.cloned.1.call-done = bf16[16384,1280]{1,0:T(8,128)(2,1)} async-done(((bf16[2048,1280]{1,0:T(8,128)(2,1)}), bf16[16384,1280]{1,0:T(8,128)(2,1)}) %all-gather.34.cloned.1.call-update) | async-done | bytes 41943056 | tf_op jit(solution)/shard_map/all_gather | solution.py:17
  1647.5 21.4 %reduce_sum.226 = bf16[2048,1280]{1,0:T(8,128)(2,1)} reduce(bf16[8,2048,1280]{2,1,0:T(8,128)(2,1)} %bitcast.208, bf16[]{:T(256)} %constant.87.clone.1), dimensions={0}, to_apply=%region_26.27 | reduce | flops 18350080 | bytes 47185920 | tf_op jit(solution)/shard_map/reduce_sum | solution.py:18
  1668.9 7.4 convert_element_type.188
  1676.3 170.3 %all-gather.36.cloned.1.call-done = bf16[10240,2048]{1,0:T(8,128)(2,1)} async-done(((bf16[1280,2048]{1,0:T(8,128)(2,1)}), bf16[10240,2048]{1,0:T(8,128)(2,1)}) %all-gather.36.cloned.1.call-update) | async-done | bytes 41943056 | tf_op jit(solution)/shard_map/all_gather | solution.py:17
  1846.6 17.2 reduce_sum.227
  1863.8 8.0 convert_element_type.190
  (248 shorter events, 50.4 us)
Async XLA Ops:
  7.2 3.0 copy-start
  7.2 6.2 copy-start.5
  7.2 6.2 copy-start.51
  7.2 37.7 %all-gather.18.cloned.1.call-start = ((), (), s32[]{:S(2)}) async-start(), calls=%async_computation.5 | async-start | bytes 1572864 | tf_op jit(solution)/shard_map/all_gather | solution.py:153
  7.3 6.1 copy-start.36
  10.1 112.2 %copy-start.57 = (f32[512]{0:T(512)}, f32[512]{0:T(512)S(1)}, u32[]{:S(2)}) copy-start(f32[512]{0:T(512)S(1)} %get-tuple-element.111) | copy-start | bytes 6148
  10.1 5.0 copy-start.67
  14.4 9.7 copy-start.73
  15.0 32.2 %copy-start.44 = (f32[512,4]{0,1:T(4,128)}, f32[512,4]{0,1:T(4,128)S(1)}, u32[]{:S(2)}) copy-start(f32[512,4]{0,1:T(4,128)S(1)} %get-tuple-element.107) | copy-start | bytes 24580
  16.2 102.4 %copy-start.61 = (f32[256]{0:T(256)}, f32[256]{0:T(256)S(1)}, u32[]{:S(2)}) copy-start(f32[256]{0:T(256)S(1)} %mul.446) | copy-start | bytes 3076
  16.5 109.8 %copy-start.26 = (f32[512,64]{0,1:T(8,128)}, f32[512,64]{0,1:T(8,128)S(1)}, u32[]{:S(2)}) copy-start(f32[512,64]{0,1:T(8,128)S(1)} %get-tuple-element.129) | copy-start | bytes 393220
  16.5 109.8 %copy-start.31 = (f32[512,64]{0,1:T(8,128)}, f32[512,64]{0,1:T(8,128)S(1)}, u32[]{:S(2)}) copy-start(f32[512,64]{0,1:T(8,128)S(1)} %get-tuple-element.130) | copy-start | bytes 393220
  20.7 89.9 %all-gather.28.cloned.1.call-start = ((), (), s32[]{:S(2)}) async-start(), calls=%async_computation.15 | async-start | bytes 4325376 | tf_op jit(solution)/shard_map/all_gather | solution.py:137
  22.4 152.3 %all-gather.20.cloned.1.call-start = ((), (), s32[]{:S(2)}) async-start(), calls=%async_computation.6 | async-start | bytes 4325376 | tf_op jit(solution)/shard_map/all_gather | solution.py:144
  24.0 308.0 %all-gather.22.cloned.1.call-start = ((), (), s32[]{:S(2)}) async-start(), calls=%async_computation.7 | async-start | bytes 10485760 | tf_op jit(solution)/shard_map/all_gather | solution.py:170
  122.3 3.2 copy-start.63
  127.2 13.6 copy-start.17
  140.8 15.0 copy-start.42
  140.8 15.5 copy-start.39
  174.7 7.2 copy-start.49
  183.6 342.8 %reduce-scatter.6.cloned.1.call-start = ((), (), s32[]{:S(2)}) async-start(), calls=%async_computation.8 | async-start | bytes 10485760 | tf_op jit(solution)/shard_map/reduce_scatter | solution.py:175
  332.0 16.7 copy-start.72
  382.5 143.9 %copy-start.12 = (bf16[512,2048]{1,0:T(8,128)(2,1)S(1)}, bf16[512,2048]{1,0:T(8,128)(2,1)}, u32[]{:S(2)}) copy-start(bf16[512,2048]{1,0:T(8,128)(2,1)} %param.16) | copy-start | bytes 6291460
  382.5 299.8 %all-gather.24.cloned.1.call-start = ((), (), s32[]{:S(2)}) async-start(), calls=%async_computation.9 | async-start | bytes 10485760 | tf_op jit(solution)/shard_map/all_gather | solution.py:182
  427.6 104.1 %copy-start.74 = (f32[128]{0:T(128)}, f32[128]{0:T(128)S(1)}, u32[]{:S(2)}) copy-start(f32[128]{0:T(128)S(1)} %broadcast_reduce_fusion) | copy-start | bytes 1540
  531.8 354.9 %reduce-scatter.8.cloned.1.call-start = ((), (), s32[]{:S(2)}) async-start(), calls=%async_computation.10 | async-start | bytes 10485760 | tf_op jit(solution)/shard_map/reduce_scatter | solution.py:187
  743.8 142.9 %copy-start.50 = (f32[2048]{0:T(1024)S(1)}, f32[2048]{0:T(1024)}, u32[]{:S(2)}) copy-start(f32[2048]{0:T(1024)} %param.26) | copy-start | bytes 24580
  743.8 142.9 %copy-start.56 = (f32[512]{0:T(512)S(1)}, f32[512]{0:T(512)}, u32[]{:S(2)}) copy-start(f32[512]{0:T(512)} %copy-done.55) | copy-start | bytes 6148
  743.9 271.7 %reduce-scatter.10.cloned.1.call-start = ((), (), s32[]{:S(2)}) async-start(), calls=%async_computation.11 | async-start | bytes 1572864 | tf_op jit(solution)/shard_map/reduce_scatter | solution.py:204
  744.6 148.6 %copy-start.66 = (f32[512]{0:T(512)S(1)}, f32[512]{0:T(512)}, u32[]{:S(2)}) copy-start(f32[512]{0:T(512)} %get-tuple-element.112) | copy-start | bytes 6148
  886.7 6.5 copy-start.2
  886.7 6.5 copy-start.13
  886.7 6.5 copy-start.22
  893.3 5.6 copy-start.28
  898.8 4.8 copy-start.10
  903.7 15.8 copy-start.40
  944.0 28.1 %copy-start.18 = (bf16[512,16,64]{0,2,1:T(8,128)(2,1)S(1)}, bf16[512,16,64]{0,2,1:T(8,128)(2,1)}, u32[]{:S(2)}) copy-start(bf16[512,16,64]{0,2,1:T(8,128)(2,1)} %copy-done.17) | copy-start | bytes 3145732
  972.1 11.0 copy-start.25
  983.1 10.2 copy-start.41
  983.1 11.3 copy-start.32
  994.4 127.8 %reduce-scatter.12.cloned.1.call-start = ((), (), s32[]{:S(2)}) async-start(), calls=%async_computation.12 | async-start | bytes 11796480 | tf_op jit(solution)/shard_map/reduce_scatter | solution.py:226
  994.5 2.8 copy-start.11
  999.6 5.3 copy-start.23
  1000.4 4.5 copy-start.16
  1000.4 4.5 copy-start.35
  1004.9 11.9 copy-start.68
  1009.3 8.9 copy-start.45
  1009.3 9.8 copy-start.7
  1015.6 2.7 copy-start.33
  1015.6 2.7 copy-start.53
  1015.6 2.7 copy-start.62
  1015.6 3.5 copy-start.59
  1019.1 3.5 copy-start.30
  1040.5 115.8 %reduce-scatter.14.cloned.1.call-start = ((), (), s32[]{:S(2)}) async-start(), calls=%async_computation.13 | async-start | bytes 1638400 | tf_op jit(solution)/shard_map/reduce_scatter | solution.py:237
  1124.8 188.7 %all-gather.26.cloned.1.call-start = ((), (), s32[]{:S(2)}) async-start(), calls=%async_computation.14 | async-start | bytes 2359296 | tf_op jit(solution)/shard_map/all_gather | solution.py:238
  1158.0 163.4 %all-gather.30.cloned.1.call-start = ((), (), s32[]{:S(2)}) async-start(), calls=%async_computation.16 | async-start | bytes 2162688 | tf_op jit(solution)/shard_map/all_gather | solution.py:242
  1159.9 287.9 %all-gather.32.cloned.1.call-start = ((), (), s32[]{:S(2)}) async-start(), calls=%async_computation.17 | async-start | bytes 47185920 | tf_op jit(solution)/shard_map/all_gather | solution.py:17
  1176.7 470.8 %all-gather.34.cloned.1.call-start = ((), (), s32[]{:S(2)}) async-start(), calls=%async_computation.18 | async-start | bytes 47185920 | tf_op jit(solution)/shard_map/all_gather | solution.py:17
  1193.5 653.1 %all-gather.36.cloned.1.call-start = ((), (), s32[]{:S(2)}) async-start(), calls=%async_computation.19 | async-start | bytes 47185920 | tf_op jit(solution)/shard_map/all_gather | solution.py:17
  1211.2 6.9 copy-start.69
  1220.8 4.3 copy-start.54
  1220.8 4.3 copy-start.70
  1220.8 86.2 %copy-start.65 = (f32[512]{0:T(512)S(1)}, f32[512]{0:T(512)}, u32[]{:S(2)}) copy-start(f32[512]{0:T(512)} %get-tuple-element.110) | copy-start | bytes 6148
  1313.6 5.8 copy-start.19
  (28 other events, 46.9 us)
Sparse Core Ops, SparseCore 0:
  20.9 24.0 all-gather.17
  48.5 62.0 all-gather.27
  114.0 60.5 all-gather.19
  183.7 148.2 all-gather.21
  382.6 143.7 reduce-scatter.5
  531.9 150.3 all-gather.23
  744.0 142.6 reduce-scatter.7
  994.5 21.0 reduce-scatter.9
  1040.6 81.5 reduce-scatter.11
  1125.1 31.1 reduce-scatter.13
  1158.9 26.9 all-gather.25
  1189.6 58.7 all-gather.29
  1251.1 196.7 all-gather.31
  1450.4 197.1 all-gather.33
  1649.4 197.1 all-gather.35
